TPU v7x, 128 devices: a whole 4x4x4 slice. The times are simulated.
128 devices in a mesh: vir: 8 (over y_hi, x), occ: 16 (over y_lo, z, core).
Axes of the slice: x: 4, y: 4 (y_hi: 2, y_lo: 2; y = y_hi * 2 + y_lo), z: 4, core: 2. Of those that a mesh axis runs over, the one named last changes fastest.
Arguments:
- amplitudes: bfloat16 [4096, 8192], P('occ', 'vir'), may hold values from -6 to 6
- ladder_integrals: bfloat16 [8192, 8192], P('occ', 'vir'), may hold values from -0.0625 to 0.0625
- crossed_integrals: bfloat16 [2, 4096, 4096], P(None, 'occ', 'vir'), may hold values from -0.09375 to 0.09375
- vir_counts: int32 [8], replicated, may hold values from 1 to 64, 480 in all
Outputs:
- residual: bfloat16 [4096, 8192], P('occ', 'vir')
Inputs may be any that keep to these rules, and one draw needn't show every extreme that they name: `vir_counts`: the counts of all 8 irreps sum to 480 and the largest is exactly 64.
All inputs are finite; a program needn't handle non-finite values.
Results may differ from a plain program's by a relative error of at most 0.004.
Values may be sent and summed in bfloat16 or wider, within the bound.
A program may use at most 128 MiB of HBM per device.

v0:
```python
import jax
import jax.numpy as jnp
from jax import lax
from jax.sharding import PartitionSpec as P

O = 64
VS = 64
NB = 2
BP = 4096


def build_mask(vir_counts):
    slot_index = jnp.arange(VS, dtype=jnp.int32)
    blocks = []
    for block_index in range(NB):
        first_act = (slot_index < vir_counts[2 * block_index]).astype(jnp.float32)
        second_act = (slot_index < vir_counts[2 * block_index + 1]).astype(jnp.float32)
        blocks.append((first_act[:, None] * second_act[None, :]).reshape(BP))
    return jnp.concatenate(blocks)


def per_device(amplitudes, ladder_integrals, crossed_integrals, vir_counts):
    local_rows = amplitudes.shape[0]
    col_width = amplitudes.shape[1]
    full_mask = build_mask(vir_counts)
    column_mask = lax.dynamic_slice_in_dim(full_mask, lax.axis_index("vir") * col_width, col_width)
    masked = amplitudes * column_mask.astype(jnp.bfloat16)[None, :]
    spread = lax.all_gather(masked, "vir", axis=1, tiled=True)
    regrouped = lax.all_to_all(spread, "occ", split_axis=1, concat_axis=0, tiled=True)
    ladder = lax.psum_scatter(
        jnp.dot(regrouped, ladder_integrals, preferred_element_type=jnp.float32),
        "occ",
        scatter_dimension=0,
        tiled=True,
    )
    occ_local = local_rows // O
    reordered = (
        spread.reshape(occ_local, O, NB, VS, VS)
        .transpose(2, 0, 3, 1, 4)
        .reshape(NB, occ_local * VS, O * VS)
    )
    crossed_cols = crossed_integrals.shape[2]
    crossed_sum = jnp.einsum(
        "gxy,gyz->gxz",
        reordered,
        lax.all_gather(crossed_integrals, "occ", axis=1, tiled=True),
        preferred_element_type=jnp.float32,
    )
    crossed_term = crossed_sum.astype(jnp.bfloat16)
    occ_cols = crossed_cols // VS
    arranged = (
        crossed_term.reshape(NB, occ_local, VS, occ_cols, VS)
        .transpose(1, 3, 0, 2, 4)
        .reshape(occ_local, occ_cols, NB * VS, VS)
    )
    returned = lax.all_to_all(arranged, "vir", split_axis=2, concat_axis=1, tiled=True)
    returned = returned.reshape(local_rows, col_width)
    total = (ladder + returned.astype(jnp.float32)) * column_mask[None, :]
    return total.astype(jnp.bfloat16)


def solution(mesh):
    in_specs = (P("occ", "vir"), P("occ", "vir"), P(None, "occ", "vir"), P())
    out_specs = P("occ", "vir")
    return jax.shard_map(
        per_device, mesh=mesh, in_specs=in_specs, out_specs=out_specs, check_vma=False
    )
```

profile of v0, /device:TPU:0, one launch (start us, length us, event | category | flops | bytes accessed | tf_op | source)
XLA Modules:
  0.0 294.8 jit_solution(6605446424760793672)
XLA Ops:
  6.5 0.0 copy-start
  6.5 0.0 all-gather.3.cloned.1.call-start
  6.5 1.4 fusion.3
  8.0 1.3 compare_convert_fusion.2
  9.3 0.1 broadcast_multiply_fusion.2
  9.3 0.1 mul.56
  9.4 1.2 compare_convert_fusion
  10.6 0.1 broadcast_multiply_fusion.1
  10.7 0.1 mul.60
  10.8 1.2 copy.16
  12.0 1.0 broadcast_multiply_fusion
  13.0 0.0 all-gather.3.cloned.1.call-update
  13.1 0.0 all-gather.5.cloned.1.call-start
  13.1 0.7 all-gather.5.cloned.1.call-update
  13.8 0.0 reduce-scatter.2.cloned.1.call-start
  13.9 73.4 %all-gather.3.cloned.1.call-done = bf16[256,8192]{0,1:T(8,128)(2,1)} async-done(((bf16[256,1024]{0,1:T(8,128)(2,1)}), bf16[256,8192]{0,1:T(8,128)(2,1)}) %all-gather.3.cloned.1.call-update) | async-done | bytes 4194320 | tf_op jit(solution)/shard_map/all_gather | solution.py:28
  87.2 82.5 %all_to_all.28 = bf16[256,16,512]{0,2,1:T(8,128)(2,1)} all-to-all(bf16[256,16,512]{0,2,1:T(8,128)(2,1)} %bitcast.27), channel_id=1, replica_groups=mesh['vir'=8,'occ'=16] {'occ'}, dimensions={1} | all-to-all | bytes 8388608 | tf_op jit(solution)/shard_map/all_to_all | solution.py:29
  169.7 6.5 %copy.17 = bf16[16,256,512]{2,1,0:T(8,128)(2,1)} copy(bf16[16,256,512]{1,2,0:T(8,128)(2,1)} %bitcast.28) | data formatting | bytes 8388608 | tf_op jit(solution)/shard_map/all_to_all | solution.py:29
  176.2 0.0 copy-done
  176.2 10.3 %fusion.4 = f32[4096,1024]{1,0:T(8,128)} fusion(bf16[4096,512]{1,0:T(8,128)(2,1)} %bitcast.30, bf16[512,1024]{1,0:T(8,128)(2,1)S(1)} %copy-done), kind=kOutput, calls=%fused_computation.15 | convolution fusion | flops 4294967296 | bytes 22020096 | tf_op jit(solution)/shard_map/dot_general | solution.py:31
  186.5 0.0 reduce-scatter.2.cloned.1.call-update
  186.5 12.9 %reshape.51 = bf16[4,64,2,64,64]{1,0,4,3,2:T(4,128)(2,1)} reshape(bf16[256,8192]{0,1:T(8,128)(2,1)} %all-gather.3.cloned.1.call-done) | data formatting | bytes 8388608 | tf_op jit(solution)/shard_map/reshape | solution.py:38
  199.5 13.8 %copy.18 = bf16[4,64,2,64,64]{4,1,3,0,2:T(8,128)(2,1)} copy(bf16[4,64,2,64,64]{1,0,4,3,2:T(4,128)(2,1)} %reshape.51) | data formatting | bytes 8388608 | tf_op jit(solution)/shard_map/reshape | solution.py:38
  213.3 12.1 %reshape.52 = bf16[2,256,4096]{2,1,0:T(8,128)(2,1)} reshape(bf16[2,4,64,64,64]{4,3,2,1,0:T(8,128)(2,1)} %bitcast.26) | data formatting | bytes 8388608 | tf_op jit(solution)/shard_map/reshape | solution.py:40
  225.4 0.0 all-gather.5.cloned.1.call-done
  225.4 7.2 %convolution_convert_fusion = bf16[2,256,512]{2,1,0:T(8,128)(2,1)S(1)} fusion(bf16[2,256,4096]{2,1,0:T(8,128)(2,1)} %reshape.52, bf16[2,4096,512]{2,1,0:T(8,128)(2,1)} %all-gather.5.cloned.1.call-done), kind=kOutput, calls=%fused_computation.1 | convolution fusion | flops 2147745792 | bytes 13107200 | tf_op jit(solution)/shard_map/gxy,gyz->gxz/dot_general | solution.py:43
  232.6 0.5 reshape.53
  233.1 1.0 copy.19
  234.1 1.1 copy.23
  235.2 0.7 reshape.57
  236.0 13.1 %all_to_all.29 = bf16[8,2,16384]{2,1,0:T(2,128)(2,1)S(1)} all-to-all(bf16[8,2,16384]{2,1,0:T(2,128)(2,1)S(1)} %reshape.57), channel_id=1, replica_groups=mesh['vir'=8,'occ'=16] {'vir'}, dimensions={0} | all-to-all | bytes 1048576 | tf_op jit(solution)/shard_map/all_to_all | solution.py:56
  249.0 0.7 reshape.58
  249.7 0.4 copy.21
  250.1 0.0 copy-start.1
  250.1 0.3 convert_bitcast_fusion
  250.4 0.2 copy.22
  250.6 1.5 reshape.55
  252.2 33.6 %reduce-scatter.2.cloned.1.call-done = f32[256,1024]{1,0:T(8,128)} async-done(((f32[4096,1024]{1,0:T(8,128)}), f32[256,1024]{1,0:T(8,128)}) %reduce-scatter.2.cloned.1.call-update) | async-done | bytes 1048592 | tf_op jit(solution)/shard_map/reduce_scatter | solution.py:30
  285.7 2.5 multiply_convert_fusion
  288.3 0.0 copy-done.1
  (1 shorter events, 0.0 us)
Async XLA Ops:
  6.5 169.6 %copy-start = (bf16[512,1024]{1,0:T(8,128)(2,1)S(1)}, bf16[512,1024]{1,0:T(8,128)(2,1)}, u32[]{:S(2)}) copy-start(bf16[512,1024]{1,0:T(8,128)(2,1)} %param.5) | copy-start | bytes 3145732
  6.5 80.7 %all-gather.3.cloned.1.call-start = ((), (), s32[]{:S(2)}) async-start(), calls=%async_computation.3 | async-start | bytes 4718592 | tf_op jit(solution)/shard_map/all_gather | solution.py:28
  13.1 212.3 %all-gather.5.cloned.1.call-start = ((), (), s32[]{:S(2)}) async-start(), calls=%async_computation.5 | async-start | bytes 8912896 | tf_op jit(solution)/shard_map/all_gather | solution.py:46
  13.8 271.9 %reduce-scatter.2.cloned.1.call-start = ((), (), s32[]{:S(2)}) async-start(), calls=%async_computation.4 | async-start | bytes 17825792 | tf_op jit(solution)/shard_map/reduce_scatter | solution.py:30
  250.1 38.2 %copy-start.1 = (bf16[512,1024]{1,0:T(8,128)(2,1)S(1)}, bf16[512,1024]{1,0:T(8,128)(2,1)}, u32[]{:S(2)}) copy-start(bf16[512,1024]{1,0:T(8,128)(2,1)} %param.5) | copy-start | bytes 3145732
Sparse Core Ops, SparseCore 0:
  13.2 74.0 all-gather.2
  88.9 91.8 all-gather.4
  186.7 99.0 reduce-scatter.1
where the time goes:
time: 296 us; the launch traced here: 295 us
  waiting for transfers between devices  108 us (36%)
  blocking collectives  95.5 us (32%)
  local copies, waits for them, and re-layouts  54.3 us (18%)
  matrix products  17.5 us (6%)
  between operations  13.2 us (4%)
  other arithmetic  6.43 us (2%)
    all_to_all x1, blocking collectives, per_device(): lax.all_to_all(spread, 'occ', split_axis=1, concat_axis=0, tiled=True)  82.5 us
    all_gather x1, waiting for transfers between devices, per_device(): spread = lax.all_gather(masked, 'vir', axis=1, tiled=True)  73.4 us
    reduce_scatter x1, waiting for transfers between devices, per_device(): lax.psum_scatter(jnp.dot(regrouped, ladder_integrals, preferred_element_t...  33.6 us
    reshape x2, local copies, waits for them, and re-layouts, per_device(): spread.reshape(occ_local, O, NB, VS, VS).transpose(2, 0, 3, 1, 4)  26.7 us
    all_to_all x1, blocking collectives, per_device(): lax.all_to_all(arranged, 'vir', split_axis=2, concat_axis=1, tiled=True)  13.1 us
    reshape x1, local copies, waits for them, and re-layouts, per_device(): reordered = spread.reshape(occ_local, O, NB, VS, VS).transpose(2, 0, 3, 1...  12.1 us
    dot_general x1, matrix products, per_device(): jnp.dot(regrouped, ladder_integrals, preferred_element_type=jnp.float32)  10.3 us
    dot_general x1, matrix products, per_device(): jnp.einsum('gxy,gyz->gxz', reordered, lax.all_gather(crossed_integrals, '...  7.19 us
  transfers between devices with their start and end apart: 3, of which 2 were waited for; matrix products, arithmetic and copies ran while one was open for 24% of the time, Pallas kernels for 0%

commit v1 on v0

--- a/solution.py
+++ b/solution.py
@@ -25,7 +25,10 @@
     full_mask = build_mask(vir_counts)
     column_mask = lax.dynamic_slice_in_dim(full_mask, lax.axis_index("vir") * col_width, col_width)
     masked = amplitudes * column_mask.astype(jnp.bfloat16)[None, :]
-    spread = lax.all_gather(masked, "vir", axis=1, tiled=True)
+    heap = []
+    for _ in range(jax.lax.axis_size("vir")):
+        heap.append(masked)
+    spread = jnp.concatenate(jax.lax.all_to_all(jnp.stack(heap), "vir", 0, 0), axis=1)
     regrouped = lax.all_to_all(spread, "occ", split_axis=1, concat_axis=0, tiled=True)
     ladder = lax.psum_scatter(
         jnp.dot(regrouped, ladder_integrals, preferred_element_type=jnp.float32),

time: 296 us -> 284 us (0.959)
  waiting for transfers between devices: 108 us -> 28.9 us
  blocking collectives: 95.5 us -> 159 us
  local copies, waits for them, and re-layouts: 54.3 us -> 57.5 us
    all_gather x1 -> x0, waiting for transfers between devices: 73.4 us -> none  [per_device(): spread = lax.all_gather(masked, 'vir', axis=1, tiled=True)]
    all_to_all x0 -> x1, blocking collectives: none -> 67.6 us  [per_device(): jax.lax.all_to_all(jnp.stack(heap), 'vir', 0, 0)]
    reshape x2 -> x1, local copies, waits for them, and re-layouts: 26.7 us -> 6.79 us  [per_device(): jnp.concatenate(jax.lax.all_to_all(jnp.stack(heap), 'vir', 0, 0), axis=1)]
    transpose x0 -> x1, local copies, waits for them, and re-layouts: none -> 12.2 us  [per_device(): reordered = spread.reshape(occ_local, O, NB, VS, VS).transpose(2, 0, 3, 1...]
    another operation x0 -> x2, local copies, waits for them, and re-layouts: none -> 12 us  [the longest x1 11.8 us: per_device(): spread.reshape(occ_local, O, NB, VS, VS).transpose(2, 0, 3, 1, 4)]
    all_to_all x1, blocking collectives: 82.5 us -> 73.7 us  [per_device(): lax.all_to_all(spread, 'occ', split_axis=1, concat_axis=0, tiled=True)]
    reduce_scatter x1, waiting for transfers between devices: 33.6 us -> 28.2 us  [per_device(): lax.psum_scatter(jnp.dot(regrouped, ladder_integrals, preferred_element_t...]
    all_to_all x1, blocking collectives: 13.1 us -> 17.9 us  [per_device(): lax.all_to_all(arranged, 'vir', split_axis=2, concat_axis=1, tiled=True)]
  transfers between devices with their start and end apart: 3 -> 2, of which waited for: 2 -> 1; matrix products, arithmetic and copies ran while one was open for 24% -> 28% of each run, Pallas kernels for 0% -> 0%
where the time goes in v1:
time: 284 us; the launch traced here: 283 us
  blocking collectives  159 us (56%)
  local copies, waits for them, and re-layouts  57.5 us (20%)
  waiting for transfers between devices  28.9 us (10%)
  matrix products  17.5 us (6%)
  between operations  13.5 us (5%)
  other arithmetic  6.57 us (2%)
    all_to_all x1, blocking collectives, per_device(): lax.all_to_all(spread, 'occ', split_axis=1, concat_axis=0, tiled=True)  73.7 us
    all_to_all x1, blocking collectives, per_device(): jax.lax.all_to_all(jnp.stack(heap), 'vir', 0, 0)  67.6 us
    reduce_scatter x1, waiting for transfers between devices, per_device(): lax.psum_scatter(jnp.dot(regrouped, ladder_integrals, preferred_element_t...  28.2 us
    all_to_all x1, blocking collectives, per_device(): lax.all_to_all(arranged, 'vir', split_axis=2, concat_axis=1, tiled=True)  17.9 us
    transpose x1, local copies, waits for them, and re-layouts, per_device(): reordered = spread.reshape(occ_local, O, NB, VS, VS).transpose(2, 0, 3, 1...  12.2 us
    reshape x1, local copies, waits for them, and re-layouts, per_device(): reordered = spread.reshape(occ_local, O, NB, VS, VS).transpose(2, 0, 3, 1...  12.2 us
    another operation x1, local copies, waits for them, and re-layouts, per_device(): spread.reshape(occ_local, O, NB, VS, VS).transpose(2, 0, 3, 1, 4)  11.8 us
    dot_general x1, matrix products, per_device(): jnp.dot(regrouped, ladder_integrals, preferred_element_type=jnp.float32)  10.3 us
  transfers between devices with their start and end apart: 2, of which 1 were waited for; matrix products, arithmetic and copies ran while one was open for 28% of the time, Pallas kernels for 0%

profile of v1, /device:TPU:0, one launch (start us, length us, event | category | flops | bytes accessed | tf_op | source)
XLA Modules:
  0.0 283.3 jit_solution(10641433144881022020)
XLA Ops:
  6.5 0.0 copy-start
  6.5 0.0 all-gather.2.cloned.1.call-start
  6.5 0.7 all-gather.2.cloned.1.call-update
  7.3 0.0 reduce-scatter.2.cloned.1.call-start
  7.3 1.5 fusion.3
  8.8 1.3 compare_convert_fusion.2
  10.1 0.1 broadcast_multiply_fusion.2
  10.1 0.1 mul.56
  10.2 1.3 compare_convert_fusion
  11.5 0.1 broadcast_multiply_fusion.1
  11.6 0.1 mul.60
  11.6 1.1 broadcast_multiply_fusion
  12.7 0.2 copy.12
  12.9 0.3 stack.2
  13.2 67.6 %all_to_all.33 = bf16[8,256,1024]{1,2,0:T(8,128)(2,1)S(1)} all-to-all(bf16[8,256,1024]{1,2,0:T(8,128)(2,1)S(1)} %stack.2), channel_id=1, replica_groups=mesh['vir'=8,'occ'=16] {'vir'}, dimensions={0} | all-to-all | bytes 8388608 | tf_op jit(solution)/shard_map/all_to_all | solution.py:31
  80.8 0.0 copy-start.2
  80.8 73.7 %all_to_all.34 = bf16[256,16,512]{0,2,1:T(8,128)(2,1)} all-to-all(bf16[256,16,512]{0,2,1:T(8,128)(2,1)S(1)} %bitcast.26), channel_id=1, replica_groups=mesh['vir'=8,'occ'=16] {'occ'}, dimensions={1} | all-to-all | bytes 8388608 | tf_op jit(solution)/shard_map/all_to_all | solution.py:32
  154.5 0.0 copy-done.2
  154.5 6.4 %copy.13 = bf16[16,256,512]{2,1,0:T(8,128)(2,1)} copy(bf16[16,256,512]{1,2,0:T(8,128)(2,1)} %bitcast.29) | data formatting | bytes 8388608 | tf_op jit(solution)/shard_map/all_to_all | solution.py:32
  160.9 0.0 copy-done
  160.9 10.3 %fusion.4 = f32[4096,1024]{1,0:T(8,128)} fusion(bf16[4096,512]{1,0:T(8,128)(2,1)} %bitcast.31, bf16[512,1024]{1,0:T(8,128)(2,1)S(1)} %copy-done), kind=kOutput, calls=%fused_computation.15 | convolution fusion | flops 4294967296 | bytes 22020096 | tf_op jit(solution)/shard_map/dot_general | solution.py:34
  171.2 0.0 reduce-scatter.2.cloned.1.call-update
  171.2 6.8 %copy.14 = bf16[256,8,1024]{2,1,0:T(8,128)(2,1)} copy(bf16[256,8,1024]{0,2,1:T(8,128)(2,1)} %bitcast.27) | data formatting | bytes 8388608 | tf_op jit(solution)/shard_map/reshape | solution.py:31
  178.0 11.8 %reshape_reshape.3 = bf16[4,64,2,64,64]{4,3,2,1,0:T(8,128)(2,1)} reshape(bf16[256,8,1024]{2,1,0:T(8,128)(2,1)} %copy.14) | data formatting | bytes 8388608 | tf_op jit(solution)/shard_map/reshape;reshape | solution.py:41
  189.7 12.2 %copy.15 = bf16[2,4,64,64,64]{4,3,2,1,0:T(8,128)(2,1)} copy(bf16[2,4,64,64,64]{4,2,0,3,1:T(8,128)(2,1)} %bitcast.28) | data formatting | bytes 8388608 | tf_op jit(solution)/shard_map/transpose | solution.py:42
  201.9 12.2 %reshape.56 = bf16[2,256,4096]{2,1,0:T(8,128)(2,1)} reshape(bf16[2,4,64,64,64]{4,3,2,1,0:T(8,128)(2,1)} %copy.15) | data formatting | bytes 8388608 | tf_op jit(solution)/shard_map/reshape | solution.py:43
  214.0 0.0 all-gather.2.cloned.1.call-done
  214.0 7.2 %convolution_convert_fusion = bf16[2,256,512]{2,1,0:T(8,128)(2,1)S(1)} fusion(bf16[2,256,4096]{2,1,0:T(8,128)(2,1)} %reshape.56, bf16[2,4096,512]{2,1,0:T(8,128)(2,1)} %all-gather.2.cloned.1.call-done), kind=kOutput, calls=%fused_computation.1 | convolution fusion | flops 2147745792 | bytes 13107200 | tf_op jit(solution)/shard_map/gxy,gyz->gxz/dot_general | solution.py:46
  221.3 0.5 reshape.57
  221.8 1.0 copy.16
  222.8 1.1 copy.20
  223.9 0.7 reshape.61
  224.6 17.9 %all_to_all.35 = bf16[8,2,16384]{2,1,0:T(2,128)(2,1)S(1)} all-to-all(bf16[8,2,16384]{2,1,0:T(2,128)(2,1)S(1)} %reshape.61), channel_id=1, replica_groups=mesh['vir'=8,'occ'=16] {'vir'}, dimensions={0} | all-to-all | bytes 1048576 | tf_op jit(solution)/shard_map/all_to_all | solution.py:59
  242.6 0.7 reshape.62
  243.2 0.4 copy.18
  243.6 0.0 copy-start.1
  243.6 0.3 convert_bitcast_fusion
  243.9 0.2 copy.19
  244.1 1.6 reshape.59
  245.7 28.2 %reduce-scatter.2.cloned.1.call-done = f32[256,1024]{1,0:T(8,128)} async-done(((f32[4096,1024]{1,0:T(8,128)}), f32[256,1024]{1,0:T(8,128)}) %reduce-scatter.2.cloned.1.call-update) | async-done | bytes 1048592 | tf_op jit(solution)/shard_map/reduce_scatter | solution.py:33
  273.9 2.5 multiply_convert_fusion
  276.4 0.0 copy-done.1
  (1 shorter events, 0.0 us)
Async XLA Ops:
  6.5 154.3 %copy-start = (bf16[512,1024]{1,0:T(8,128)(2,1)S(1)}, bf16[512,1024]{1,0:T(8,128)(2,1)}, u32[]{:S(2)}) copy-start(bf16[512,1024]{1,0:T(8,128)(2,1)} %param.5) | copy-start | bytes 3145732
  6.5 207.5 %all-gather.2.cloned.1.call-start = ((), (), s32[]{:S(2)}) async-start(), calls=%async_computation.5 | async-start | bytes 8912896 | tf_op jit(solution)/shard_map/all_gather | solution.py:49
  7.3 266.7 %reduce-scatter.2.cloned.1.call-start = ((), (), s32[]{:S(2)}) async-start(), calls=%async_computation.4 | async-start | bytes 17825792 | tf_op jit(solution)/shard_map/reduce_scatter | solution.py:33
  80.8 73.7 %copy-start.2 = (bf16[8,256,1024]{1,2,0:T(8,128)(2,1)}, bf16[8,256,1024]{1,2,0:T(8,128)(2,1)S(1)}, u32[]{:S(2)}) copy-start(bf16[8,256,1024]{1,2,0:T(8,128)(2,1)S(1)} %all_to_all.33) | copy-start | bytes 12582916
  243.6 32.8 %copy-start.1 = (bf16[512,1024]{1,0:T(8,128)(2,1)S(1)}, bf16[512,1024]{1,0:T(8,128)(2,1)}, u32[]{:S(2)}) copy-start(bf16[512,1024]{1,0:T(8,128)(2,1)} %param.5) | copy-start | bytes 3145732
Sparse Core Ops, SparseCore 0:
  9.0 130.9 all-gather.1
  171.3 102.5 reduce-scatter.1
